TPU v7x, 256 devices: a whole 4x4x8 slice. The times are simulated.
256 devices in a mesh: req: 32 (over y, z), head: 8 (over x, core).
Axes of the slice: x: 4, y: 4, z: 8, core: 2. Of those that a mesh axis runs over, the one named last changes fastest.
Arguments:
- tokens: bfloat16 [256, 1024], P('req'), may hold values from -6 to 6
- lengths: int32 [256], P('req'), may hold values from 1 to 512, as said below
- slot_owner: int32 [256], P('req'), may hold values from 0 to 255, as said below
- positions: int32 [256], P('req'), may hold values from 0 to 8191
- variates: int32 [256], P('req'), may hold values from 0 to 7
- cache_variates: int32 [256, 512], P('req'), may hold values from 0 to 7
- kv_cache: bfloat16 [2, 2, 256, 512, 1024], P(None, None, 'req', None, 'head'), may hold values from -6 to 6
- attn_gain: float32 [2, 1024], replicated, may hold values from 0.1 to 1.9
- ffn_gain: float32 [2, 1024], replicated, may hold values from 0.1 to 1.9
- qkv_weight: bfloat16 [2, 1024, 3072], P(None, None, 'head'), may hold values from -0.1875 to 0.1875
- out_weight: bfloat16 [2, 1024, 1024], P(None, 'head'), may hold values from -0.1875 to 0.1875
- gate_up_weight: bfloat16 [2, 2, 1024, 4096], P(None, None, None, 'head'), may hold values from -0.1875 to 0.1875
- down_weight: bfloat16 [2, 4096, 1024], P(None, 'head'), may hold values from -0.09375 to 0.09375
- variate_bias: float32 [2, 2, 16], P(None, None, 'head'), may hold values from -2 to 300
Outputs:
- next_states: bfloat16 [256, 1024], P(('req', 'head'))
Inputs may be any that keep to these rules, and one draw needn't show every extreme that they name: `lengths`: live cache positions of each request; the largest is exactly 512 in every draw. `slot_owner`: each request is held in exactly one slot; taken in an order of non-increasing length, the requests fill slot t of every req index in turn t = 0, 1, ..., the req indices in rising order on even turns and in falling order on odd ones; no two slots of one req index hold requests of the same device of next_states (the same 1 request).
All inputs are finite; a program needn't handle non-finite values.
Results may differ from a plain program's by a relative error of at most 0.02.
Values may be sent and summed in bfloat16 or wider, within the bound.
A program may use at most 64 MiB of HBM per device.

v0:
```python
import jax
import jax.numpy as jnp
from jax import lax
from jax.sharding import PartitionSpec as P

HD = 64
LAYERS = 2
neg_fill = -1e30


def rms_scale(stream, gain_row):
    return stream * lax.rsqrt(jnp.mean(stream * stream, axis=-1, keepdims=True) + 1e-06) * gain_row


def rotary(vectors, time_ids):
    half_width = vectors.shape[-1] // 2
    frequency = 10000.0 ** (-2.0 * jnp.arange(half_width, dtype=jnp.float32) / vectors.shape[-1])
    angles = time_ids.astype(jnp.float32)[:, None, None] * frequency[None, None, :]
    cosine = jnp.cos(angles)
    sine_part = jnp.sin(angles)
    front_half = vectors[..., :half_width]
    back_half = vectors[..., half_width:]
    return jnp.concatenate(
        [front_half * cosine - back_half * sine_part, front_half * sine_part + back_half * cosine],
        axis=-1,
    )


def attend(
    queries,
    key_new,
    value_new,
    cached_keys,
    cached_values,
    cache_var,
    cache_lengths,
    variate_ids,
    same_bias,
    diff_bias,
):
    row_count, cache_len, width = cached_keys.shape
    local_heads = queries.shape[1]
    score_scale = HD ** (-0.5)
    diagonal_mask = jnp.eye(local_heads, dtype=jnp.bfloat16)
    q_block = (queries[:, :, :, None] * diagonal_mask[None, :, None, :]).reshape(
        row_count, local_heads * HD, local_heads
    )
    raw_scores = jnp.einsum(
        "rcf,rfh->rch", cached_keys, q_block, preferred_element_type=jnp.float32
    )
    score_bias = jnp.where(
        (cache_var == variate_ids[:, None])[:, :, None],
        same_bias[None, None, :],
        diff_bias[None, None, :],
    )
    scores = raw_scores * score_scale + score_bias
    live_mask = jnp.arange(cache_len, dtype=jnp.int32)[None, :] < cache_lengths[:, None]
    scores = jnp.where(live_mask[:, :, None], scores, neg_fill)
    self_score = (
        jnp.sum(queries.astype(jnp.float32) * key_new.astype(jnp.float32), axis=-1) * score_scale
        + same_bias[None, :]
    )
    row_top = jnp.maximum(jnp.max(scores, axis=1), self_score)
    weights = jnp.exp(scores - row_top[:, None, :])
    self_weight = jnp.exp(self_score - row_top)
    denominator = jnp.sum(weights, axis=1) + self_weight
    probs_bf16 = (weights / denominator[:, None, :]).astype(jnp.bfloat16)
    self_prob = (self_weight / denominator).astype(jnp.bfloat16)
    mixed_full = jnp.einsum(
        "rch,rcf->rhf", probs_bf16, cached_values, preferred_element_type=jnp.float32
    )
    mask_float = diagonal_mask.astype(jnp.float32)
    mixed_heads = jnp.sum(
        mixed_full.reshape(row_count, local_heads, local_heads, HD) * mask_float[None, :, :, None],
        axis=2,
    )
    mixed_heads = mixed_heads + self_prob.astype(jnp.float32)[:, :, None] * value_new.astype(
        jnp.float32
    )
    return mixed_heads.reshape(row_count, local_heads * HD).astype(jnp.bfloat16)


def per_device(
    tokens,
    lengths,
    slot_owner,
    positions,
    variates,
    cache_variates,
    kv_cache,
    attn_gain,
    ffn_gain,
    qkv_weight,
    out_weight,
    gate_up_weight,
    down_weight,
    variate_bias,
):
    head_count = lax.axis_size("head")
    head_place = lax.axis_index("head")
    slot_count = slot_owner.shape[0]
    token_share = slot_count // head_count
    all_lengths, all_times, all_variates, all_owners = (
        lax.all_gather(lengths, "req", axis=0, tiled=True),
        lax.all_gather(positions, "req", axis=0, tiled=True),
        lax.all_gather(variates, "req", axis=0, tiled=True),
        lax.all_gather(slot_owner, "req", axis=0, tiled=True),
    )
    all_tokens = lax.all_gather(tokens, "req", axis=0, tiled=True)
    slot_tokens = jnp.take(all_tokens, slot_owner, axis=0).astype(jnp.float32)
    cache_lengths = jnp.take(all_lengths, slot_owner)
    time_ids = jnp.take(all_times, slot_owner)
    variate_ids = jnp.take(all_variates, slot_owner)
    residual = lax.dynamic_slice_in_dim(slot_tokens, head_place * token_share, token_share, 0)
    local_heads = kv_cache.shape[-1] // HD
    for layer_index in range(LAYERS):
        if layer_index == 0:
            normed = rms_scale(slot_tokens, attn_gain[0]).astype(jnp.bfloat16)
        else:
            normed = lax.all_gather(
                rms_scale(residual, attn_gain[layer_index]).astype(jnp.bfloat16),
                "head",
                axis=0,
                tiled=True,
            )
        projected = jnp.dot(normed, qkv_weight[layer_index], preferred_element_type=jnp.float32)
        projected = projected.reshape(slot_count, local_heads, 3, HD)
        queries = rotary(projected[:, :, 0], time_ids).astype(jnp.bfloat16)
        key_new = rotary(projected[:, :, 1], time_ids).astype(jnp.bfloat16)
        value_new = projected[:, :, 2].astype(jnp.bfloat16)
        attended = attend(
            queries,
            key_new,
            value_new,
            kv_cache[layer_index, 0],
            kv_cache[layer_index, 1],
            cache_variates,
            cache_lengths,
            variate_ids,
            variate_bias[layer_index, 0],
            variate_bias[layer_index, 1],
        )
        out_partial = jnp.dot(attended, out_weight[layer_index], preferred_element_type=jnp.float32)
        residual = residual + lax.psum_scatter(
            out_partial.astype(jnp.bfloat16), "head", scatter_dimension=0, tiled=True
        ).astype(jnp.float32)
        ffn_input = lax.all_gather(
            rms_scale(residual, ffn_gain[layer_index]).astype(jnp.bfloat16),
            "head",
            axis=0,
            tiled=True,
        )
        paired = jnp.einsum(
            "rd,gdf->grf",
            ffn_input,
            gate_up_weight[layer_index],
            preferred_element_type=jnp.float32,
        )
        hidden = (jax.nn.silu(paired[0]) * paired[1]).astype(jnp.bfloat16)
        ffn_partial = jnp.dot(hidden, down_weight[layer_index], preferred_element_type=jnp.float32)
        residual = residual + lax.psum_scatter(
            ffn_partial.astype(jnp.bfloat16), "head", scatter_dimension=0, tiled=True
        ).astype(jnp.float32)
    final_rows = residual.astype(jnp.bfloat16)
    own_place = lax.axis_index("req") * head_count + head_place
    request_ids = own_place * token_share + jnp.arange(token_share, dtype=jnp.int32)
    matches = all_owners[None, :] == request_ids[:, None]
    slot_index = jnp.sum(
        jnp.where(matches, jnp.arange(all_owners.shape[0], dtype=jnp.int32)[None, :], 0), axis=1
    )
    everything = lax.all_gather(final_rows, ("req", "head"), axis=0, tiled=True)
    return jnp.take(everything, slot_index, axis=0)


def solution(mesh):
    return jax.shard_map(
        per_device,
        mesh=mesh,
        in_specs=(
            P("req", None),
            P("req"),
            P("req"),
            P("req"),
            P("req"),
            P("req", None),
            P(None, None, "req", None, "head"),
            P(),
            P(),
            P(None, None, "head"),
            P(None, "head", None),
            P(None, None, None, "head"),
            P(None, "head", None),
            P(None, None, "head"),
        ),
        out_specs=P(("req", "head"), None),
        check_vma=False,
    )
```

profile of v0, /device:TPU:1, one launch (start us, length us, event | category | flops | bytes accessed | tf_op | source)
XLA Modules:
  0.0 306.1 jit_solution(2157831063779013560)
XLA Ops:
  0.0 1.3 dynamic-slice.4
  2.0 0.9 dynamic-update-slice.1
  2.8 0.8 dynamic-update-slice.4
  3.7 0.8 dynamic-update-slice.2
  4.5 0.8 dynamic-update-slice.3
  5.3 20.3 %all-reduce.8 = (s32[256]{0:T(256)S(1)}, s32[256]{0:T(256)S(1)}, s32[256]{0:T(256)S(1)}, s32[256]{0:T(256)S(1)}) all-reduce(s32[256]{0:T(256)S(1)} %dynamic-update-slice.1, s32[256]{0:T(256)S(1)} %dynamic-update-slice.4, s32[256]{0:T(256)S(1)} %dynamic-update-slice.2, s32[256]{0:T(256)S(1)} %dynamic-update-slice.3), channel_id=1, replica_groups=mesh['req'=32,'head'=8] {'req'}, use_global_device_ids=true, to_apply=%add | all-reduce | flops 1024 | bytes 8192
  25.6 0.6 fusion.84
  28.2 0.8 slice_bitcast_fusion.7
  28.9 0.7 compare_select_fusion
  29.6 0.6 gather_fusion.2
  30.3 0.7 select_convert_fusion
  30.9 0.6 gather_fusion.1
  31.6 0.6 gather_fusion.3
  32.2 0.8 iota_compare_fusion
  33.3 1.6 slice_bitcast_fusion
  34.9 0.3 copy.67
  35.2 35.6 %all_gather.28 = bf16[256,1024]{1,0:T(8,128)(2,1)S(1)} all-gather(bf16[8,1024]{1,0:T(8,128)(2,1)S(1)} %copy-done.2), channel_id=1, replica_groups=mesh['req'=32,'head'=8] {'req'}, dimensions={0}, use_global_device_ids=true | all-gather | bytes 540672 | tf_op jit(solution)/shard_map/all_gather | solution.py:109
  70.8 0.6 gather_fusion
  71.4 0.2 multiply_reduce_fusion
  71.6 0.4 fusion.39
  72.4 1.7 fusion.94
  74.1 0.2 multiply_reduce_fusion.4
  74.4 0.2 fusion.36
  74.6 1.5 fusion.23
  76.7 36.7 %all-reduce.4 = bf16[8,1024]{1,0:T(8,128)(2,1)S(1)} all-reduce(bf16[8,1024]{1,0:T(8,128)(2,1)S(1)} %convolution_convert_fusion.3), channel_id=2, replica_groups=mesh['req'=32,'head'=8] {'head'}, use_global_device_ids=true, to_apply=%region_6.8.clone | all-reduce | flops 8192 | bytes 32768
  113.4 0.6 dynamic-slice.9
  114.1 1.3 multiply_reduce_fusion.7
  116.1 16.3 %all-gather = bf16[8,1,1024]{2,1,0:T(2,128)(2,1)S(1)} all-gather(bf16[1,1,1024]{2,1,0:T(2,128)(2,1)S(1)} %convert_bitcast_fusion.2), channel_id=1, replica_groups=mesh['req'=32,'head'=8] {'head'}, dimensions={0}, use_global_device_ids=true | all-gather | bytes 18432 | tf_op jit(solution)/shard_map/all_gather | solution.py:147
  132.4 2.0 fusion.6
  134.3 1.5 convolution_convert_fusion.2
  135.8 20.4 %all-reduce.5 = bf16[8,1024]{1,0:T(8,128)(2,1)S(1)} all-reduce(bf16[8,1024]{1,0:T(8,128)(2,1)S(1)} %convolution_convert_fusion.2), channel_id=3, replica_groups=mesh['req'=32,'head'=8] {'head'}, use_global_device_ids=true, to_apply=%region_8.10.clone | all-reduce | flops 8192 | bytes 32768
  156.2 1.3 multiply_reduce_fusion.6
  157.5 0.3 copy.75
  158.5 16.3 %all-gather.1 = bf16[8,1,1024]{2,1,0:T(2,128)(2,1)S(1)} all-gather(bf16[1,1,1024]{2,1,0:T(2,128)(2,1)S(1)} %convert_bitcast_fusion.1), channel_id=1, replica_groups=mesh['req'=32,'head'=8] {'head'}, dimensions={0}, use_global_device_ids=true | all-gather | bytes 18432 | tf_op jit(solution)/shard_map/all_gather | solution.py:120
  174.8 0.4 fusion.43
  175.4 1.8 fusion.95
  177.3 0.2 multiply_reduce_fusion.3
  177.5 0.2 fusion.37
  177.7 1.5 fusion.19
  179.9 20.4 %all-reduce.6 = bf16[8,1024]{1,0:T(8,128)(2,1)S(1)} all-reduce(bf16[8,1024]{1,0:T(8,128)(2,1)S(1)} %convolution_convert_fusion.1), channel_id=4, replica_groups=mesh['req'=32,'head'=8] {'head'}, use_global_device_ids=true, to_apply=%region_14.16.clone | all-reduce | flops 8192 | bytes 32768
  200.3 1.3 multiply_reduce_fusion.5
  202.2 16.3 %all-gather.2 = bf16[8,1,1024]{2,1,0:T(2,128)(2,1)S(1)} all-gather(bf16[1,1,1024]{2,1,0:T(2,128)(2,1)S(1)} %convert_bitcast_fusion), channel_id=1, replica_groups=mesh['req'=32,'head'=8] {'head'}, dimensions={0}, use_global_device_ids=true | all-gather | bytes 18432 | tf_op jit(solution)/shard_map/all_gather | solution.py:147
  218.5 2.0 fusion.9
  220.5 0.3 convolution_convert_fusion
  220.7 20.4 %all-reduce.7 = bf16[8,1024]{1,0:T(8,128)(2,1)S(1)} all-reduce(bf16[8,1024]{1,0:T(8,128)(2,1)S(1)} %convolution_convert_fusion), channel_id=5, replica_groups=mesh['req'=32,'head'=8] {'head'}, use_global_device_ids=true, to_apply=%region_16.18.clone | all-reduce | flops 8192 | bytes 32768
  241.1 0.7 fusion.70
  241.8 63.7 %all-gather.3 = bf16[256,1,1024]{2,1,0:T(2,128)(2,1)S(1)} all-gather(bf16[1,1,1024]{2,1,0:T(2,128)(2,1)S(1)} %fusion.70), channel_id=1, replica_groups=mesh['req'=32,'head'=8] {'req','head'}, dimensions={0}, use_global_device_ids=true | all-gather | bytes 526336 | tf_op jit(solution)/shard_map/all_gather | solution.py:171
  305.5 0.6 fusion.65
  (62 shorter events, 2.5 us)
Async XLA Ops:
  0.0 71.6 %slice-start = ((f32[2,1024]{1,0:T(2,128)}), f32[1,1024]{1,0:T(1,128)S(1)}, s32[]{:S(2)}) async-start(f32[2,1024]{1,0:T(2,128)} %param.23), calls=%async_computation | async-start | bytes 8192 | tf_op jit(solution)/shard_map/slice | solution.py:118
  0.0 35.2 %copy-start.2 = (bf16[8,1024]{1,0:T(8,128)(2,1)S(1)}, bf16[8,1024]{1,0:T(8,128)(2,1)}, u32[]{:S(2)}) copy-start(bf16[8,1024]{1,0:T(8,128)(2,1)} %param.16) | copy-start | bytes 49156
  33.3 43.3 %copy-start = (bf16[2,128,1024]{2,1,0:T(8,128)(2,1)S(1)}, bf16[2,128,1024]{2,1,0:T(8,128)(2,1)}, u32[]{:S(2)}) copy-start(bf16[2,128,1024]{2,1,0:T(8,128)(2,1)} %param.26) | copy-start | bytes 1572868
  33.3 80.1 %copy-start.5 = (u32[256]{0:T(256)S(1)}, u32[256]{0:T(256)}, u32[]{:S(2)}) copy-start(u32[256]{0:T(256)} %constant.146) | copy-start | bytes 3076
  33.3 82.7 %copy-start.3 = (f32[2,1024]{1,0:T(2,128)S(1)}, f32[2,1024]{1,0:T(2,128)}, u32[]{:S(2)}) copy-start(f32[2,1024]{1,0:T(2,128)} %param.24) | copy-start | bytes 24580
  72.4 86.1 %copy-start.1 = (f32[2,1024]{1,0:T(2,128)S(1)}, f32[2,1024]{1,0:T(2,128)}, u32[]{:S(2)}) copy-start(f32[2,1024]{1,0:T(2,128)} %param.23) | copy-start | bytes 24580
  175.2 45.3 %copy-start.4 = (bf16[2,512,1024]{2,1,0:T(8,128)(2,1)S(1)}, bf16[2,512,1024]{2,1,0:T(8,128)(2,1)}, u32[]{:S(2)}) copy-start(bf16[2,512,1024]{2,1,0:T(8,128)(2,1)} %param.28) | copy-start | bytes 6291460
where the time goes:
time: 307 us; the launch traced here: 306 us
  blocking collectives  266 us (87%)
  matrix products  13.4 us (4%)
  local copies, waits for them, and re-layouts  11.9 us (4%)
  other arithmetic  9.74 us (3%)
  between operations  4.82 us (2%)
    unnamed x5, blocking collectives  118 us
    all_gather x1, blocking collectives, per_device(): everything = lax.all_gather(final_rows, ('req', 'head'), axis=0, tiled=True)  63.7 us
    all_gather x1, blocking collectives, per_device(): all_tokens = lax.all_gather(tokens, 'req', axis=0, tiled=True)  35.6 us
    all_gather x2, blocking collectives, per_device(): lax.all_gather(rms_scale(residual, ffn_gain[layer_index]).astype(jnp.bflo...  32.6 us
    all_gather x1, blocking collectives, per_device(): lax.all_gather(rms_scale(residual, attn_gain[layer_index]).astype(jnp.bfl...  16.3 us

commit v1 on v0

--- a/solution.py
+++ b/solution.py
@@ -106,7 +106,16 @@
         lax.all_gather(variates, "req", axis=0, tiled=True),
         lax.all_gather(slot_owner, "req", axis=0, tiled=True),
     )
-    all_tokens = lax.all_gather(tokens, "req", axis=0, tiled=True)
+    pass_space_on = lambda z_in, peer_axis: jnp.concatenate(
+        jax.lax.all_to_all(
+            jnp.stack(jax.lax.axis_size(peer_axis) * [z_in]),
+            axis_name=peer_axis,
+            split_axis=0,
+            concat_axis=0,
+        ),
+        axis=0,
+    )
+    all_tokens = pass_space_on(tokens, "req")
     slot_tokens = jnp.take(all_tokens, slot_owner, axis=0).astype(jnp.float32)
     cache_lengths = jnp.take(all_lengths, slot_owner)
     time_ids = jnp.take(all_times, slot_owner)

time: 307 us -> 271 us (0.88)
  blocking collectives: 266 us -> 216 us
  starting transfers between devices: 0 us -> 12.2 us
    all_gather x1 -> x0, blocking collectives: 35.6 us -> none  [per_device(): all_tokens = lax.all_gather(tokens, 'req', axis=0, tiled=True)]
    unnamed x5, blocking collectives: 118 us -> 104 us
    all_to_all x0 -> x1, starting transfers between devices: none -> 12.2 us  [per_device(): jax.lax.all_to_all(jnp.stack(jax.lax.axis_size(peer_axis) * [z_in]), axis...]
  transfers between devices with their start and end apart: 0 -> 1, of which waited for: 0 -> 0; matrix products, arithmetic and copies ran while one was open for 0% -> 4% of each run, Pallas kernels for 0% -> 0%
where the time goes in v1:
time: 271 us
  blocking collectives  216 us (80%)
  matrix products  14.4 us (5%)
  local copies, waits for them, and re-layouts  13.8 us (5%)
  starting transfers between devices  12.2 us (5%)
  other arithmetic  9.17 us (3%)
  between operations  5.08 us (2%)
    unnamed x5, blocking collectives  104 us
    all_gather x1, blocking collectives, per_device(): everything = lax.all_gather(final_rows, ('req', 'head'), axis=0, tiled=True)  62.7 us
    all_gather x2, blocking collectives, per_device(): lax.all_gather(rms_scale(residual, ffn_gain[layer_index]).astype(jnp.bflo...  32.6 us
    all_gather x1, blocking collectives, per_device(): lax.all_gather(rms_scale(residual, attn_gain[layer_index]).astype(jnp.bfl...  16.3 us
    all_to_all x1, starting transfers between devices, per_device(): jax.lax.all_to_all(jnp.stack(jax.lax.axis_size(peer_axis) * [z_in]), axis...  12.2 us
  transfers between devices with their start and end apart: 1, of which 0 were waited for; matrix products, arithmetic and copies ran while one was open for 4% of the time, Pallas kernels for 0%

profile of v1, /device:TPU:1, one launch (start us, length us, event | category | flops | bytes accessed | tf_op | source)
XLA Modules:
  0.0 270.5 jit_solution(6071292300538363986)
XLA Ops:
  0.0 1.6 stack.2
  1.6 12.2 %all-to-all-start = ((bf16[32,8,1024]{2,1,0:T(8,128)(2,1)}), bf16[32,8,1024]{2,1,0:T(8,128)(2,1)}, u32[]{:S(2)}, u32[]{:S(2)}) async-start(bf16[32,8,1024]{2,1,0:T(8,128)(2,1)} %stack.2), calls=%async_computation | async-start | bytes 1048576 | tf_op jit(solution)/shard_map/all_to_all | solution.py:110
  13.8 0.7 compare_select_fusion
  14.5 1.3 dynamic-slice.4
  16.4 0.9 dynamic-update-slice.1
  17.3 0.8 dynamic-update-slice.2
  18.1 0.8 dynamic-update-slice.3
  19.0 0.8 dynamic-update-slice.4
  19.8 19.1 %all-reduce.8 = (s32[256]{0:T(256)S(1)}, s32[256]{0:T(256)S(1)}, s32[256]{0:T(256)S(1)}, s32[256]{0:T(256)S(1)}) all-reduce(s32[256]{0:T(256)S(1)} %dynamic-update-slice.1, s32[256]{0:T(256)S(1)} %dynamic-update-slice.4, s32[256]{0:T(256)S(1)} %dynamic-update-slice.2, s32[256]{0:T(256)S(1)} %dynamic-update-slice.3), channel_id=1, replica_groups=mesh['req'=32,'head'=8] {'req'}, use_global_device_ids=true, to_apply=%add | all-reduce | flops 1024 | bytes 8192
  38.9 0.6 gather_fusion.2
  39.5 0.7 select_convert_fusion
  40.2 1.5 slice_bitcast_fusion
  41.7 0.6 fusion.84
  42.4 0.3 copy.67
  42.7 0.6 gather_fusion.1
  43.3 0.6 gather_fusion.3
  44.3 0.3 copy.75
  46.5 0.6 dynamic-slice.9
  47.4 1.7 gather_fusion
  49.1 0.2 multiply_reduce_fusion
  49.3 0.4 fusion.39
  49.9 0.2 multiply_reduce_fusion.4
  50.3 1.7 fusion.94
  52.0 0.2 fusion.36
  52.2 1.5 fusion.23
  54.2 0.1 convolution_convert_fusion.3
  54.3 24.1 %all-reduce.4 = bf16[8,1024]{1,0:T(8,128)(2,1)S(1)} all-reduce(bf16[8,1024]{1,0:T(8,128)(2,1)S(1)} %convolution_convert_fusion.3), channel_id=2, replica_groups=mesh['req'=32,'head'=8] {'head'}, use_global_device_ids=true, to_apply=%region_6.8.clone | all-reduce | flops 8192 | bytes 32768
  78.4 1.3 multiply_reduce_fusion.7
  80.5 16.3 %all-gather = bf16[8,1,1024]{2,1,0:T(2,128)(2,1)S(1)} all-gather(bf16[1,1,1024]{2,1,0:T(2,128)(2,1)S(1)} %convert_bitcast_fusion.2), channel_id=1, replica_groups=mesh['req'=32,'head'=8] {'head'}, dimensions={0}, use_global_device_ids=true | all-gather | bytes 18432 | tf_op jit(solution)/shard_map/all_gather | solution.py:156
  96.8 2.0 fusion.6
  98.8 1.5 convolution_convert_fusion.2
  100.2 20.4 %all-reduce.5 = bf16[8,1024]{1,0:T(8,128)(2,1)S(1)} all-reduce(bf16[8,1024]{1,0:T(8,128)(2,1)S(1)} %convolution_convert_fusion.2), channel_id=3, replica_groups=mesh['req'=32,'head'=8] {'head'}, use_global_device_ids=true, to_apply=%region_8.10.clone | all-reduce | flops 8192 | bytes 32768
  120.6 1.3 multiply_reduce_fusion.6
  122.7 16.3 %all-gather.1 = bf16[8,1,1024]{2,1,0:T(2,128)(2,1)S(1)} all-gather(bf16[1,1,1024]{2,1,0:T(2,128)(2,1)S(1)} %convert_bitcast_fusion.1), channel_id=1, replica_groups=mesh['req'=32,'head'=8] {'head'}, dimensions={0}, use_global_device_ids=true | all-gather | bytes 18432 | tf_op jit(solution)/shard_map/all_gather | solution.py:129
  139.0 0.4 fusion.43
  139.5 0.2 multiply_reduce_fusion.3
  139.9 1.7 fusion.95
  141.6 0.2 fusion.37
  141.9 1.5 fusion.19
  144.0 20.4 %all-reduce.6 = bf16[8,1024]{1,0:T(8,128)(2,1)S(1)} all-reduce(bf16[8,1024]{1,0:T(8,128)(2,1)S(1)} %convolution_convert_fusion.1), channel_id=4, replica_groups=mesh['req'=32,'head'=8] {'head'}, use_global_device_ids=true, to_apply=%region_14.16.clone | all-reduce | flops 8192 | bytes 32768
  164.4 1.3 multiply_reduce_fusion.5
  166.5 16.3 %all-gather.2 = bf16[8,1,1024]{2,1,0:T(2,128)(2,1)S(1)} all-gather(bf16[1,1,1024]{2,1,0:T(2,128)(2,1)S(1)} %convert_bitcast_fusion), channel_id=1, replica_groups=mesh['req'=32,'head'=8] {'head'}, dimensions={0}, use_global_device_ids=true | all-gather | bytes 18432 | tf_op jit(solution)/shard_map/all_gather | solution.py:156
  182.8 2.0 fusion.9
  184.7 1.5 convolution_convert_fusion
  186.2 20.4 %all-reduce.7 = bf16[8,1024]{1,0:T(8,128)(2,1)S(1)} all-reduce(bf16[8,1024]{1,0:T(8,128)(2,1)S(1)} %convolution_convert_fusion), channel_id=5, replica_groups=mesh['req'=32,'head'=8] {'head'}, use_global_device_ids=true, to_apply=%region_16.18.clone | all-reduce | flops 8192 | bytes 32768
  206.6 0.7 fusion.70
  207.3 62.7 %all-gather.3 = bf16[256,1,1024]{2,1,0:T(2,128)(2,1)S(1)} all-gather(bf16[1,1,1024]{2,1,0:T(2,128)(2,1)S(1)} %fusion.70), channel_id=1, replica_groups=mesh['req'=32,'head'=8] {'req','head'}, dimensions={0}, use_global_device_ids=true | all-gather | bytes 526336 | tf_op jit(solution)/shard_map/all_gather | solution.py:180
  269.9 0.6 fusion.65
  (64 shorter events, 2.5 us)
Async XLA Ops:
  1.6 45.8 %all-to-all-start = ((bf16[32,8,1024]{2,1,0:T(8,128)(2,1)}), bf16[32,8,1024]{2,1,0:T(8,128)(2,1)}, u32[]{:S(2)}, u32[]{:S(2)}) async-start(bf16[32,8,1024]{2,1,0:T(8,128)(2,1)} %stack.2), calls=%async_computation | async-start | bytes 1048576 | tf_op jit(solution)/shard_map/all_to_all | solution.py:110
  13.7 32.8 %copy-start.5 = (u32[256]{0:T(256)S(1)}, u32[256]{0:T(256)}, u32[]{:S(2)}) copy-start(u32[256]{0:T(256)} %constant.146) | copy-start | bytes 3076
  13.8 33.4 %copy-start.4 = (f32[2,2,2]{2,1,0:T(2,128)S(1)}, f32[2,2,2]{2,1,0:T(2,128)}, u32[]{:S(2)}) copy-start(f32[2,2,2]{2,1,0:T(2,128)} %param.29) | copy-start | bytes 100
  13.8 33.5 %copy-start.2 = (s32[8,512]{1,0:T(8,128)S(1)}, s32[8,512]{1,0:T(8,128)}, u32[]{:S(2)}) copy-start(s32[8,512]{1,0:T(8,128)} %param.21) | copy-start | bytes 49156
  13.8 35.6 %slice-start = ((f32[2,1024]{1,0:T(2,128)}), f32[1,1024]{1,0:T(1,128)S(1)}, s32[]{:S(2)}) async-start(f32[2,1024]{1,0:T(2,128)} %param.23), calls=%async_computation.1 | async-start | bytes 8192 | tf_op jit(solution)/shard_map/slice | solution.py:127
  42.4 38.1 %copy-start.3 = (f32[2,1024]{1,0:T(2,128)S(1)}, f32[2,1024]{1,0:T(2,128)}, u32[]{:S(2)}) copy-start(f32[2,1024]{1,0:T(2,128)} %param.24) | copy-start | bytes 24580
  42.7 11.5 %copy-start = (bf16[2,128,1024]{2,1,0:T(8,128)(2,1)S(1)}, bf16[2,128,1024]{2,1,0:T(8,128)(2,1)}, u32[]{:S(2)}) copy-start(bf16[2,128,1024]{2,1,0:T(8,128)(2,1)} %param.26) | copy-start | bytes 1572868
  44.6 78.1 %copy-start.1 = (f32[2,1024]{1,0:T(2,128)S(1)}, f32[2,1024]{1,0:T(2,128)}, u32[]{:S(2)}) copy-start(f32[2,1024]{1,0:T(2,128)} %param.23) | copy-start | bytes 24580
